TPU v7x, 1024 devices: a whole 8x8x8 slice. The times are simulated.
1024 devices in a mesh: mat: 8 (over x), gr: 64 (over z, y), gc: 2 (over core).
Axes of the slice: x: 8, y: 8, z: 8, core: 2. Of those that a mesh axis runs over, the one named last changes fastest.
Arguments:
- iterate: bfloat16 [2, 64, 32, 7168], P(None, 'gr', ('mat', 'gc')), may hold values from -3 to 3
Outputs:
- next_iterate: bfloat16 [2, 2048, 7168], P(None, 'gr', ('mat', 'gc'))
All inputs are finite; a program needn't handle non-finite values.
Results may differ from a plain program's by a relative error of at most 0.0055.
Values may be sent and summed in bfloat16 or wider, within the bound.
A program may use at most 32 MiB of HBM per device.

v0:
```python
import jax
import jax.numpy as jnp
from jax import lax
from jax.sharding import PartitionSpec as P

N = 7168


linear_coef = 3.4445
cubic_coef = -4.775
quintic_coef = 2.0315


def body(iterate):
    regrouped = lax.all_to_all(iterate, ("mat", "gc"), split_axis=3, concat_axis=2, tiled=True)
    row_block = regrouped[:, 0]
    panel_rows = lax.all_gather(row_block, "gr", axis=1, tiled=True)
    total_rows = panel_rows.shape[1]
    groups = lax.axis_size(("mat", "gc"))
    gram_width = total_rows // groups
    inv_cols = 1.0 / N
    partial_value = jnp.einsum(
        "irc,ijc->irj", row_block, panel_rows, preferred_element_type=jnp.float32
    )
    gram_rows = (lax.psum(partial_value, ("mat", "gc")) * inv_cols).astype(jnp.bfloat16)
    own_block = lax.dynamic_slice_in_dim(
        gram_rows, lax.axis_index(("mat", "gc")) * gram_width, gram_width, 2
    )
    square = jnp.einsum(
        "irk,ikj->irj",
        gram_rows,
        lax.all_gather(own_block, "gr", axis=1, tiled=True),
        preferred_element_type=jnp.float32,
    )
    poly_block = (cubic_coef * own_block.astype(jnp.float32) + quintic_coef * square).astype(
        jnp.bfloat16
    )
    mixed_sum = jnp.einsum(
        "irk,ikc->irc",
        lax.all_gather(poly_block, ("mat", "gc"), axis=2, tiled=True),
        panel_rows,
        preferred_element_type=jnp.float32,
    )
    result = linear_coef * row_block.astype(jnp.float32) + mixed_sum
    return result.astype(jnp.bfloat16)


def solution(mesh):
    return jax.shard_map(
        body,
        mesh=mesh,
        in_specs=(P(None, "gr", ("mat", "gc"), None),),
        out_specs=P(None, "gr", ("mat", "gc")),
        check_vma=False,
    )
```

profile of v0, /device:TPU:1, one launch (start us, length us, event | category | flops | bytes accessed | tf_op | source)
XLA Modules:
  0.0 399.3 jit_solution(8747316973261831834)
XLA Ops:
  6.5 0.0 all-gather.3.cloned.1.call-start
  6.5 7.6 %copy.8 = bf16[2,1,2,7168]{2,0,1,3:T(2,128)(2,1)} copy(bf16[2,1,2,7168]{3,2,1,0:T(2,128)(2,1)} %param.1) | data formatting | bytes 114688 | tf_op args[0]
  14.1 8.5 %reshape.1 = bf16[16,2,896]{2,1,0:T(2,128)(2,1)S(1)} reshape(bf16[7168,1,2,2]{3,2,1,0:T(2,128)(2,1)} %bitcast.13) | data formatting | bytes 114688
  22.6 24.2 %all_to_all.15 = bf16[16,2,896]{2,1,0:T(2,128)(2,1)S(1)} all-to-all(bf16[16,2,896]{2,1,0:T(2,128)(2,1)S(1)} %reshape.1), channel_id=1, replica_groups=mesh['mat'=8,'gr'=64,'gc'=2] {'mat','gc'}, dimensions={0} | all-to-all | bytes 114688 | tf_op jit(solution)/shard_map/all_to_all | solution.py:15
  46.9 8.9 %reshape.2 = bf16[7168,1,2,2]{3,2,1,0:T(2,128)(2,1)} reshape(bf16[16,2,896]{2,1,0:T(2,128)(2,1)S(1)} %all_to_all.15) | data formatting | bytes 114688
  55.7 6.0 %copy.11 = bf16[2,1,2,16,448]{4,3,2,0,1:T(8,128)(2,1)S(1)} copy(bf16[2,1,2,16,448]{2,0,4,3,1:T(2,128)(2,1)} %bitcast.12) | data formatting | bytes 114688 | tf_op jit(solution)/shard_map/all_to_all | solution.py:15
  61.7 0.1 copy.10
  61.8 0.7 squeeze.3
  62.5 0.0 copy-start
  62.5 0.0 all-gather.3.cloned.1.call-update
  62.5 0.0 all-reduce.2.cloned.1.call-start
  62.6 88.8 %all-gather.3.cloned.1.call-done = bf16[2,2048,448]{2,1,0:T(8,128)(2,1)} async-done(((bf16[2,32,448]{2,1,0:T(8,128)(2,1)}), bf16[2,2048,448]{2,1,0:T(8,128)(2,1)}) %all-gather.3.cloned.1.call-update) | async-done | bytes 3670032 | tf_op jit(solution)/shard_map/all_gather | solution.py:17
  151.3 4.3 %fusion.3 = f32[2,32,2048]{2,1,0:T(8,128)} fusion(bf16[2,32,448]{2,1,0:T(8,128)(2,1)} %squeeze.3, bf16[2,2048,448]{2,1,0:T(8,128)(2,1)} %all-gather.3.cloned.1.call-done), kind=kOutput, calls=%fused_computation.7 | convolution fusion | flops 117440512 | bytes 4251648 | tf_op jit(solution)/shard_map/irc,ijc->irj/dot_general | solution.py:22
  155.7 0.0 all-reduce.2.cloned.1.call-update
  155.7 0.0 all-gather.5.cloned.1.call-start
  155.7 120.5 %all-reduce.2.cloned.1.call-done = f32[2,32,2048]{2,1,0:T(8,128)} async-done(((f32[2,32,2048]{2,1,0:T(8,128)}), f32[2,32,2048]{2,1,0:T(8,128)}) %all-reduce.2.cloned.1.call-update) | async-done | bytes 524304 | tf_op jit(solution)/shard_map/psum | solution.py:25
  276.3 1.1 multiply_convert_fusion
  277.4 0.6 constant_dynamic-slice_fusion
  278.0 0.0 all-gather.5.cloned.1.call-update
  278.0 87.1 %all-gather.5.cloned.1.call-done = bf16[2,2048,128]{2,1,0:T(8,128)(2,1)} async-done(((bf16[2,32,128]{2,1,0:T(8,128)(2,1)}), bf16[2,2048,128]{2,1,0:T(8,128)(2,1)}) %all-gather.5.cloned.1.call-update) | async-done | bytes 1048592 | tf_op jit(solution)/shard_map/all_gather | solution.py:32
  365.1 1.5 fusion.2
  366.6 22.5 %all_gather.11 = bf16[2,32,2048]{2,1,0:T(8,128)(2,1)S(1)} all-gather(bf16[2,32,128]{2,1,0:T(8,128)(2,1)S(1)} %fusion.2), channel_id=1, replica_groups=mesh['mat'=8,'gr'=64,'gc'=2] {'mat','gc'}, dimensions={2}, use_global_device_ids=true | all-gather | bytes 278528 | tf_op jit(solution)/shard_map/all_gather | solution.py:40
  389.1 0.0 copy-done
  389.1 3.6 fusion
Async XLA Ops:
  6.5 144.8 %all-gather.3.cloned.1.call-start = ((), (), s32[]{:S(2)}) async-start(), calls=%async_computation.1 | async-start | bytes 4259840 | tf_op jit(solution)/shard_map/all_gather | solution.py:17
  62.5 326.6 %copy-start = (bf16[2,32,448]{2,1,0:T(8,128)(2,1)S(1)}, bf16[2,32,448]{2,1,0:T(8,128)(2,1)}, u32[]{:S(2)}) copy-start(bf16[2,32,448]{2,1,0:T(8,128)(2,1)} %squeeze.3) | copy-start | bytes 172036
  62.5 213.7 %all-reduce.2.cloned.1.call-start = ((), (), s32[]{:S(2)}) async-start(), calls=%async_computation.2 | async-start | bytes 1048576 | tf_op jit(solution)/shard_map/psum | solution.py:25
  155.7 209.4 %all-gather.5.cloned.1.call-start = ((), (), s32[]{:S(2)}) async-start(), calls=%async_computation.3 | async-start | bytes 1064960 | tf_op jit(solution)/shard_map/all_gather | solution.py:32
Sparse Core Ops, SparseCore 0:
  62.6 88.6 all-gather.2
  155.8 120.4 all-reduce.1
  281.1 83.9 all-gather.4
where the time goes:
time: 400 us; the launch traced here: 399 us
  waiting for transfers between devices  296 us (74%)
  blocking collectives  46.7 us (12%)
  local copies, waits for them, and re-layouts  32.3 us (8%)
  between operations  13.1 us (3%)
  matrix products  9.45 us (2%)
    psum x1, waiting for transfers between devices, body(): lax.psum(partial_value, ('mat', 'gc')) * inv_cols  121 us
    all_gather x1, waiting for transfers between devices, body(): panel_rows = lax.all_gather(row_block, 'gr', axis=1, tiled=True)  88.8 us
    all_gather x1, waiting for transfers between devices, body(): lax.all_gather(own_block, 'gr', axis=1, tiled=True)  87.1 us
    unnamed x5, local copies, waits for them, and re-layouts  25 us
    all_to_all x1, blocking collectives, body(): lax.all_to_all(iterate, ('mat', 'gc'), split_axis=3, concat_axis=2, tiled...  24.2 us
    all_gather x1, blocking collectives, body(): lax.all_gather(poly_block, ('mat', 'gc'), axis=2, tiled=True)  22.5 us
  transfers between devices with their start and end apart: 3, of which 3 were waited for; matrix products, arithmetic and copies ran while one was open for 0% of the time, Pallas kernels for 0%

commit v1 on v0

v1 whole, which is shorter than its diff:
```python
import functools

import jax
import jax.numpy as jnp
from jax import lax
from jax.experimental import pallas as pl
from jax.experimental.pallas import tpu as pltpu
from jax.sharding import PartitionSpec as P

MESH = pl.DeviceIdType.MESH

linear_coef = 3.4445
cubic_coef = -4.775
quintic_coef = 2.0315


def column_cuts(width):
    cut = (width // 128 + 1) // 2 * 128
    return ((0, cut), (cut, width - cut))


class Ring:
    def __init__(self, size, me, neighbour, view, send, recv):
        self.size, self.me, self.neighbour, self.view = size, me, neighbour, view
        self.send, self.recv = send, recv

    def steps(self):
        return self.size // 2

    def has(self, step, way, q):
        return step < self.steps() or (step == self.steps() and q == way)

    def copy(self, step, way, q, index):
        turn = 1 if way == 0 else self.size - 1
        ref = self.view(lax.rem(index, self.size), q)
        return pltpu.make_async_remote_copy(
            src_ref=ref,
            dst_ref=ref,
            send_sem=self.send.at[step - 1, way, q],
            recv_sem=self.recv.at[step - 1, way, q],
            device_id={"gr": self.neighbour(lax.rem(self.me + turn, self.size))},
            device_id_type=MESH,
        )

    def sent(self, step, way, q):
        back = step - 1 if way == 1 else self.size - (step - 1)
        return self.copy(step, way, q, self.me + back)

    def arriving(self, step, way, q):
        back = step if way == 1 else self.size - step
        return self.copy(step, way, q, self.me + back)


def run_rings(rings):
    for q in range(2):
        for ring in rings:
            for way in range(2):
                if ring.has(1, way, q):
                    ring.sent(1, way, q).start()
    for step in range(1, max(r.steps() for r in rings) + 1):
        for q in range(2):
            for ring in rings:
                for way in range(2):
                    if ring.has(step, way, q):
                        ring.arriving(step, way, q).wait_recv()
                        if ring.has(step + 1, way, q):
                            ring.sent(step + 1, way, q).start()


def drain_rings(rings):
    for ring in rings:
        for step in range(1, ring.steps() + 1):
            for q in range(2):
                for way in range(2):
                    if ring.has(step, way, q):
                        ring.sent(step, way, q).wait_send()


def kernel(
    nx, nz, ny, total_cols,
    in_ref, out_ref,
    pieces, assembled, panel, partial, partial_in, gram_cols, gram_row, poly_row, swap_out, swap_in,
    a2a_send, a2a_recv, local_sem,
    pa_send, pa_recv, pb_send, pb_recv, ga_send, ga_recv, gb_send, gb_recv,
    rs_send, rs_recv, gx_send, gx_recv, px_send, px_recv, sw_send, sw_recv,
):
    x = lax.axis_index("mat")
    g = lax.axis_index("gr")
    c = lax.axis_index("gc")
    z, y = lax.div(g, ny), lax.rem(g, ny)
    rpd = in_ref.shape[1]
    block_rows, width = panel.shape[2], panel.shape[3]
    half_rows = block_rows // 2
    gram_width = gram_row.shape[2]

    def x_at(dx):
        return lax.rem(x + dx, nx)

    others = [(dx, dc) for dx in range(nx) for dc in range(2) if (dx, dc) != (0, 0)]
    barrier = pltpu.get_barrier_semaphore()
    for dx, dc in others:
        pl.semaphore_signal(
            barrier, inc=1, device_id={"mat": x_at(dx), "gc": lax.rem(c + dc, 2)}, device_id_type=MESH
        )
    for turn in (1, ny - 1):
        pl.semaphore_signal(
            barrier, inc=1, device_id={"gr": z * ny + lax.rem(y + turn, ny)}, device_id_type=MESH
        )
    for turn in (1, nz - 1):
        pl.semaphore_signal(
            barrier, inc=1, device_id={"gr": lax.rem(z + turn, nz) * ny + y}, device_id_type=MESH
        )
    pl.semaphore_wait(barrier, len(others) + 4)

    def exchange(dx, dc):
        to_x, to_c = x_at(dx), lax.rem(c + dc, 2)
        return pltpu.make_async_remote_copy(
            src_ref=in_ref.at[to_c, :, pl.ds(pl.multiple_of(to_x * width, 128), width)],
            dst_ref=pieces.at[x, c],
            send_sem=a2a_send.at[dx, dc],
            recv_sem=a2a_recv.at[dx, dc],
            device_id={"mat": to_x, "gc": to_c},
            device_id_type=MESH,
        )

    for dx, dc in others:
        exchange(dx, dc).start()
    own = pltpu.make_async_copy(
        in_ref.at[c, :, pl.ds(pl.multiple_of(x * width, 128), width)], pieces.at[x, c], local_sem
    )
    own.start()
    own.wait()
    for dx, dc in others:
        exchange(dx, dc).wait_recv()
    for k in range(nx):
        for core in range(2):
            row = (k * 2 + core) * rpd
            assembled[row : row + rpd, :] = pieces[k, core].astype(jnp.float32)
    panel[z, y] = assembled[...].astype(jnp.bfloat16)

    def gathers(buf, cuts, a_send, a_recv, b_send, b_recv):
        def rows(half):
            return pl.ds(half * half_rows, half_rows)

        def along_y(yy):
            return z * ny + yy

        def along_z(zz):
            return zz * ny + y

        first = [
            Ring(ny, y, along_y, lambda i, q: buf.at[z, i, rows(0), pl.ds(*cuts[q])], a_send.at[0], a_recv.at[0]),
            Ring(nz, z, along_z, lambda i, q: buf.at[i, y, rows(1), pl.ds(*cuts[q])], a_send.at[1], a_recv.at[1]),
        ]
        second = [
            Ring(nz, z, along_z, lambda i, q: buf.at[i, :, rows(0), pl.ds(*cuts[q])], b_send.at[0], b_recv.at[0]),
            Ring(ny, y, along_y, lambda i, q: buf.at[:, i, rows(1), pl.ds(*cuts[q])], b_send.at[1], b_recv.at[1]),
        ]
        return first, second

    panel_a, panel_b = gathers(panel, column_cuts(width), pa_send, pa_recv, pb_send, pb_recv)
    run_rings(panel_a)
    run_rings(panel_b)

    def contribute(dx):
        to_x = x_at(dx)
        return pltpu.make_async_remote_copy(
            src_ref=partial.at[to_x],
            dst_ref=partial_in.at[x],
            send_sem=rs_send.at[dx],
            recv_sem=rs_recv.at[dx],
            device_id={"mat": to_x},
            device_id_type=MESH,
        )

    far_first = sorted(range(1, nx), key=lambda dx: -min(dx, nx - dx))
    block = panel[z, y]
    for dx in far_first + [0]:
        to_x = x_at(dx)
        value = lax.dot_general(
            block,
            panel[to_x].reshape(ny * block_rows, width),
            (((1,), (1,)), ((), ())),
            preferred_element_type=jnp.float32,
        )
        if dx:
            partial[to_x] = value
            contribute(dx).start()
        else:
            gram_sum = value
    for dx in far_first:
        contribute(dx).wait_recv()
    for dx in range(1, nx):
        gram_sum = gram_sum + partial_in[x_at(dx)]
    gram = (gram_sum * (1.0 / total_cols)).astype(jnp.bfloat16)
    gram_row[x] = gram
    gram_cols[z, y] = gram

    def spread(buf, send, recv, dx, at):
        return pltpu.make_async_remote_copy(
            src_ref=buf.at[at],
            dst_ref=buf.at[at],
            send_sem=send.at[dx],
            recv_sem=recv.at[dx],
            device_id={"mat": x_at(dx)},
            device_id_type=MESH,
        )

    for dx in far_first:
        spread(gram_row, gx_send, gx_recv, dx, x).start()
    gram_a, gram_b = gathers(gram_cols, column_cuts(gram_width), ga_send, ga_recv, gb_send, gb_recv)
    run_rings(gram_a)
    run_rings(gram_b)
    for dx in far_first:
        spread(gram_row, gx_send, gx_recv, dx, x_at(nx - dx)).wait_recv()

    square = jnp.zeros((block_rows, gram_width), jnp.float32)
    for k in range(nx):
        square = square + jnp.dot(
            gram_row[k],
            gram_cols[k].reshape(ny * block_rows, gram_width),
            preferred_element_type=jnp.float32,
        )
    poly_row[x] = (cubic_coef * gram.astype(jnp.float32) + quintic_coef * square).astype(jnp.bfloat16)
    for dx in far_first:
        spread(poly_row, px_send, px_recv, dx, x).start()
    for dx in far_first:
        spread(poly_row, px_send, px_recv, dx, x_at(nx - dx)).wait_recv()

    mixed = jnp.zeros((block_rows, width), jnp.float32)
    for k in range(nx):
        mixed = mixed + jnp.dot(
            poly_row[k], panel[k].reshape(ny * block_rows, width), preferred_element_type=jnp.float32
        )
    result = linear_coef * panel[z, y].astype(jnp.float32) + mixed
    halves = [
        result[:, : width // 2].astype(jnp.bfloat16),
        result[:, width // 2 :].astype(jnp.bfloat16),
    ]
    for core in range(2):

        @pl.when(c == core)
        def _():
            out_ref[core] = halves[core]
            swap_out[...] = halves[1 - core]

    swap = pltpu.make_async_remote_copy(
        src_ref=swap_out,
        dst_ref=swap_in,
        send_sem=sw_send,
        recv_sem=sw_recv,
        device_id={"gc": 1 - c},
        device_id_type=MESH,
    )
    swap.start()
    swap.wait_recv()
    for core in range(2):

        @pl.when(c == core)
        def _():
            out_ref[1 - core] = swap_in[...]

    swap.wait_send()
    for dx, dc in others:
        exchange(dx, dc).wait_send()
    for rings in (panel_a, panel_b, gram_a, gram_b):
        drain_rings(rings)
    for dx in far_first:
        contribute(dx).wait_send()
        spread(gram_row, gx_send, gx_recv, dx, x).wait_send()
        spread(poly_row, px_send, px_recv, dx, x).wait_send()


def solution(mesh):
    nx, groups = mesh.shape["mat"], mesh.shape["gr"]
    nz = nx
    ny = groups // nz

    def body(iterate):
        mats, _, rpd, total_cols = iterate.shape
        block_rows = rpd * nx * 2
        width = total_cols // nx
        gram_width = ny * block_rows
        dma = pltpu.SemaphoreType.DMA
        y_or_z = max(ny, nz) // 2
        ring_sems = [dma((2, y_or_z, 2, 2))] * 2
        return pl.pallas_call(
            functools.partial(kernel, nx, nz, ny, total_cols),
            out_shape=jax.ShapeDtypeStruct((mats, block_rows, width // 2), jnp.bfloat16),
            in_specs=[pl.BlockSpec(memory_space=pltpu.VMEM)],
            out_specs=pl.BlockSpec(memory_space=pltpu.VMEM),
            scratch_shapes=[
                pltpu.VMEM((nx, 2, rpd, width), jnp.bfloat16),
                pltpu.VMEM((block_rows, width), jnp.float32),
                pltpu.VMEM((nz, ny, block_rows, width), jnp.bfloat16),
                pltpu.VMEM((nx, block_rows, gram_width), jnp.float32),
                pltpu.VMEM((nx, block_rows, gram_width), jnp.float32),
                pltpu.VMEM((nz, ny, block_rows, gram_width), jnp.bfloat16),
                pltpu.VMEM((nx, block_rows, gram_width), jnp.bfloat16),
                pltpu.VMEM((nx, block_rows, gram_width), jnp.bfloat16),
                pltpu.VMEM((block_rows, width // 2), jnp.bfloat16),
                pltpu.VMEM((block_rows, width // 2), jnp.bfloat16),
                dma((nx, 2)),
                dma((nx, 2)),
                dma,
            ]
            + ring_sems * 4
            + [dma((nx,))] * 6
            + [dma, dma],
            compiler_params=pltpu.CompilerParams(collective_id=0, has_side_effects=True),
        )(iterate.reshape(mats, rpd, total_cols))

    return jax.shard_map(
        body,
        mesh=mesh,
        in_specs=(P(None, "gr", ("mat", "gc"), None),),
        out_specs=P(None, "gr", ("mat", "gc")),
        check_vma=False,
    )
```

time: 400 us -> 111 us (0.28)
  waiting for transfers between devices: 296 us -> 0 us
  Pallas kernels: 0 us -> 109 us
  blocking collectives: 46.7 us -> 0 us
  local copies, waits for them, and re-layouts: 32.3 us -> 1.47 us
  between operations: 13.1 us -> 0.01 us
  matrix products: 9.45 us -> 0 us
    all_gather x2 -> x0, waiting for transfers between devices: 176 us -> none  [the longest x1 88.8 us: body(): panel_rows = lax.all_gather(row_block, 'gr', axis=1, tiled=True)]
    psum x1 -> x0, waiting for transfers between devices: 121 us -> none  [body(): lax.psum(partial_value, ('mat', 'gc')) * inv_cols]
    pallas_call x0 -> x1, Pallas kernels: none -> 109 us  [body(): pl.pallas_call(functools.partial(kernel, nx, nz, ny, total_cols), out_sha...]
    all_to_all x1 -> x0, blocking collectives: 24.2 us -> none  [body(): lax.all_to_all(iterate, ('mat', 'gc'), split_axis=3, concat_axis=2, tiled...]
    unnamed x5 -> x1, local copies, waits for them, and re-layouts: 25 us -> 1.47 us
    all_gather x1 -> x0, blocking collectives: 22.5 us -> none  [body(): lax.all_gather(poly_block, ('mat', 'gc'), axis=2, tiled=True)]
    dot_general x3 -> x0, matrix products: 9.45 us -> none  [the longest x1 4.32 us: body(): jnp.einsum('irc,ijc->irj', row_block, panel_rows, preferred_element_type=...]
    all_to_all x2 -> x0, local copies, waits for them, and re-layouts: 6.07 us -> none  [body(): lax.all_to_all(iterate, ('mat', 'gc'), split_axis=3, concat_axis=2, tiled...]
  transfers between devices with their start and end apart: 3 -> 0, of which waited for: 3 -> 0; matrix products, arithmetic and copies ran while one was open for 0% -> 0% of each run, Pallas kernels for 0% -> 0%
where the time goes in v1:
time: 111 us
  Pallas kernels  109 us (98%)
  local copies, waits for them, and re-layouts  1.47 us (1%)
    pallas_call x1, Pallas kernels, body(): pl.pallas_call(functools.partial(kernel, nx, nz, ny, total_cols), out_sha...  109 us

profile of v1, /device:TPU:1, one launch (start us, length us, event | category | flops | bytes accessed | tf_op | source)
XLA Modules:
  0.0 110.9 jit_solution(14166464483223373454)
XLA Ops:
  0.0 109.4 %shard_map.17 = bf16[2,32,448]{2,1,0:T(8,128)(2,1)} custom-call(bf16[2,2,7168]{2,1,0:T(2,128)(2,1)} %bitcast.1), custom_call_target="tpu_custom_call" | custom-call | tf_op jit(solution)/shard_map/pallas_call | solution.py:287
  109.4 1.5 %copy.3 = bf16[2,32,448]{2,1,0:T(8,128)(2,1)} copy(bf16[2,32,448]{2,1,0:T(8,128)(2,1)} %shard_map.17) | data formatting | bytes 114688

commit v2 on v1

v2 whole, which is shorter than its diff:
```python
import functools

import jax
import jax.numpy as jnp
from jax import lax
from jax.experimental import pallas as pl
from jax.experimental.pallas import tpu as pltpu
from jax.sharding import PartitionSpec as P

MESH = pl.DeviceIdType.MESH

linear_coef = 3.4445
cubic_coef = -4.775
quintic_coef = 2.0315


class Gather:
    def __init__(self, buf, sizes, line, line_send, line_recv, send, recv):
        self.buf, self.sizes, self.line = buf, sizes, line
        self.line_send, self.line_recv, self.send, self.recv = line_send, line_recv, send, recv
        self.half_rows = buf.shape[2] // 2

    def view(self, half, first, second):
        rows = pl.ds(half * self.half_rows, self.half_rows)
        return self.buf.at[(second, first, rows) if half == 0 else (first, second, rows)]

    def first_size(self, half):
        return self.sizes[1 - half]

    def second_size(self, half):
        return self.sizes[half]

    def first_copy(self, half, d):
        size = self.first_size(half)
        return pltpu.make_async_remote_copy(
            src_ref=self.view(half, 0, 0),
            dst_ref=self.view(half, size - d, 0),
            send_sem=self.line_send.at[half, d],
            recv_sem=self.line_recv.at[half, d],
            device_id={"gr": self.line[1 - half][d]},
            device_id_type=MESH,
        )

    def start_first(self):
        for half in range(2):
            for d in nearest_last(self.first_size(half)):
                self.first_copy(half, d).start()

    def wait_first(self, half, low, high):
        size = self.first_size(half)
        for place in range(max(low, 1), high):
            self.first_copy(half, size - place).wait_recv()

    def end_first(self):
        for half in range(2):
            for d in range(1, self.first_size(half)):
                self.first_copy(half, d).wait_send()


class RingGather(Gather):
    def chunks(self, half):
        size = self.first_size(half)
        cuts = [(0, 1), (1, size // 2), (size // 2, size)]
        return [(k, low, high) for k, (low, high) in enumerate(cuts) if low < high]

    def steps(self, half):
        return self.second_size(half) // 2

    def has(self, half, step, way, k):
        return step < self.steps(half) or (step == self.steps(half) and way == k // 2)

    def copy(self, half, step, way, chunk):
        size, (k, low, high) = self.second_size(half), chunk
        source, target = (step - 1, step) if way else ((size - step + 1) % size, size - step)
        return pltpu.make_async_remote_copy(
            src_ref=self.view(half, pl.ds(low, high - low), source),
            dst_ref=self.view(half, pl.ds(low, high - low), target),
            send_sem=self.send.at[half, step - 1, way, k],
            recv_sem=self.recv.at[half, step - 1, way, k],
            device_id={"gr": self.line[half][size - 1 if way else 1]},
            device_id_type=MESH,
        )

    def all(self):
        for half in range(2):
            for step in range(1, self.steps(half) + 1):
                for way in range(2):
                    for chunk in self.chunks(half):
                        if self.has(half, step, way, chunk[0]):
                            yield half, step, way, chunk

    def run(self):
        def start(half, step, way, chunk):
            if self.has(half, step, way, chunk[0]):
                self.copy(half, step, way, chunk).start()

        for half in range(2):
            for way in range(2):
                start(half, 1, way, self.chunks(half)[0])
        self.start_first()
        for n in range(1, 3):
            for half in range(2):
                if n < len(self.chunks(half)):
                    chunk = self.chunks(half)[n]
                    self.wait_first(half, chunk[1], chunk[2])
                    for way in range(2):
                        start(half, 1, way, chunk)
        for step in range(1, max(self.steps(0), self.steps(1)) + 1):
            for n in range(3):
                for half in range(2):
                    for way in range(2):
                        if n < len(self.chunks(half)) and self.has(half, step, way, self.chunks(half)[n][0]):
                            chunk = self.chunks(half)[n]
                            self.copy(half, step, way, chunk).wait_recv()
                            start(half, step + 1, way, chunk)

    def end(self):
        self.end_first()
        for one in self.all():
            self.copy(*one).wait_send()


class LineGather(Gather):
    def copy(self, half, d):
        size = self.second_size(half)
        return pltpu.make_async_remote_copy(
            src_ref=self.view(half, pl.ds(0, self.first_size(half)), 0),
            dst_ref=self.view(half, pl.ds(0, self.first_size(half)), size - d),
            send_sem=self.send.at[half, d],
            recv_sem=self.recv.at[half, d],
            device_id={"gr": self.line[half][d]},
            device_id_type=MESH,
        )

    def run(self):
        self.start_first()
        for half in range(2):
            self.wait_first(half, 1, self.first_size(half))
            for d in nearest_last(self.second_size(half)):
                self.copy(half, d).start()
        for half in range(2):
            for d in nearest_last(self.second_size(half)):
                self.copy(half, d).wait_recv()

    def end(self):
        self.end_first()
        for half in range(2):
            for d in range(1, self.second_size(half)):
                self.copy(half, d).wait_send()


def nearest_last(size):
    return sorted(range(1, size), key=lambda d: -min(d, size - d))


def kernel(
    nx, nz, ny, total_cols,
    in_ref, out_ref,
    pieces, assembled, panel, partial, partial_in, gram_cols, gram_row, poly_row, swap_out, swap_in,
    a2a_send, a2a_recv, local_sem,
    pa_send, pa_recv, pb_send, pb_recv, ga_send, ga_recv, gb_send, gb_recv,
    rs_send, rs_recv, gx_send, gx_recv, px_send, px_recv, sw_send, sw_recv,
):
    x = lax.axis_index("mat")
    g = lax.axis_index("gr")
    c = lax.axis_index("gc")
    z, y = lax.div(g, ny), lax.rem(g, ny)
    rpd = in_ref.shape[1]
    block_rows, width = panel.shape[2], panel.shape[3]
    gram_width = gram_row.shape[2]
    x_at = [lax.rem(x + dx, nx) for dx in range(nx)]
    c_at = [c, 1 - c]
    line = (
        [lax.rem(z + dz, nz) * ny + y for dz in range(nz)],
        [z * ny + lax.rem(y + dy, ny) for dy in range(ny)],
    )
    place_z = [lax.rem(x_at[dx] + nz - z, nz) for dx in range(nx)]
    place_y = [lax.rem(k + ny - y, ny) for k in range(ny)]

    def row_block(buf, dx):
        return jnp.concatenate([buf[place_z[dx], place_y[k]] for k in range(ny)], axis=0)

    others = [(dx, dc) for dx in nearest_last(nx) + [0] for dc in range(2) if (dx, dc) != (0, 0)]
    barrier = pltpu.get_barrier_semaphore()
    for dx, dc in others:
        pl.semaphore_signal(
            barrier, inc=1, device_id={"mat": x_at[dx], "gc": c_at[dc]}, device_id_type=MESH
        )
    for axis in range(2):
        for to in line[axis][1:]:
            pl.semaphore_signal(barrier, inc=1, device_id={"gr": to}, device_id_type=MESH)
    pl.semaphore_wait(barrier, len(others) + nz - 1 + ny - 1)

    def exchange(dx, dc):
        to_x, to_c = x_at[dx], c_at[dc]
        return pltpu.make_async_remote_copy(
            src_ref=in_ref.at[to_c, :, pl.ds(pl.multiple_of(to_x * width, 128), width)],
            dst_ref=pieces.at[x, c],
            send_sem=a2a_send.at[dx, dc],
            recv_sem=a2a_recv.at[dx, dc],
            device_id={"mat": to_x, "gc": to_c},
            device_id_type=MESH,
        )

    for dx, dc in others:
        exchange(dx, dc).start()
    own = pltpu.make_async_copy(
        in_ref.at[c, :, pl.ds(pl.multiple_of(x * width, 128), width)], pieces.at[x, c], local_sem
    )
    own.start()
    own.wait()
    for dx, dc in others:
        exchange(dx, dc).wait_recv()
    for k in range(nx):
        for core in range(2):
            row = (k * 2 + core) * rpd
            assembled[row : row + rpd, :] = pieces[k, core].astype(jnp.float32)
    block = assembled[...].astype(jnp.bfloat16)
    panel[0, 0] = block

    panel_gather = RingGather(panel, (nz, ny), line, pa_send, pa_recv, pb_send, pb_recv)
    panel_gather.run()

    def contribute(dx):
        return pltpu.make_async_remote_copy(
            src_ref=partial.at[dx],
            dst_ref=partial_in.at[nx - dx],
            send_sem=rs_send.at[dx],
            recv_sem=rs_recv.at[dx],
            device_id={"mat": x_at[dx]},
            device_id_type=MESH,
        )

    far_first = nearest_last(nx)
    for dx in far_first + [0]:
        value = lax.dot_general(
            block, row_block(panel, dx), (((1,), (1,)), ((), ())), preferred_element_type=jnp.float32
        )
        if dx:
            partial[dx] = value
            contribute(dx).start()
        else:
            gram_sum = value
    for dx in far_first:
        contribute(dx).wait_recv()
        gram_sum = gram_sum + partial_in[nx - dx]
    gram = (gram_sum * (1.0 / total_cols)).astype(jnp.bfloat16)
    gram_row[0] = gram
    gram_cols[0, 0] = gram

    def spread(buf, send, recv, dx):
        return pltpu.make_async_remote_copy(
            src_ref=buf.at[0],
            dst_ref=buf.at[nx - dx],
            send_sem=send.at[dx],
            recv_sem=recv.at[dx],
            device_id={"mat": x_at[dx]},
            device_id_type=MESH,
        )

    for dx in far_first:
        spread(gram_row, gx_send, gx_recv, dx).start()
    gram_gather = LineGather(gram_cols, (nz, ny), line, ga_send, ga_recv, gb_send, gb_recv)
    gram_gather.run()
    for dx in far_first:
        spread(gram_row, gx_send, gx_recv, dx).wait_recv()

    square = jnp.zeros((block_rows, gram_width), jnp.float32)
    for dx in range(nx):
        square = square + jnp.dot(gram_row[dx], row_block(gram_cols, dx), preferred_element_type=jnp.float32)
    poly_row[0] = (cubic_coef * gram.astype(jnp.float32) + quintic_coef * square).astype(jnp.bfloat16)
    for dx in far_first:
        spread(poly_row, px_send, px_recv, dx).start()

    mixed = jnp.zeros((block_rows, width), jnp.float32)
    for dx in [0] + far_first[::-1]:
        if dx:
            spread(poly_row, px_send, px_recv, nx - dx).wait_recv()
        mixed = mixed + jnp.dot(poly_row[dx], row_block(panel, dx), preferred_element_type=jnp.float32)
    result = linear_coef * block.astype(jnp.float32) + mixed
    halves = [
        result[:, : width // 2].astype(jnp.bfloat16),
        result[:, width // 2 :].astype(jnp.bfloat16),
    ]
    for core in range(2):

        @pl.when(c == core)
        def _():
            out_ref[core] = halves[core]
            swap_out[...] = halves[1 - core]

    swap = pltpu.make_async_remote_copy(
        src_ref=swap_out,
        dst_ref=swap_in,
        send_sem=sw_send,
        recv_sem=sw_recv,
        device_id={"gc": 1 - c},
        device_id_type=MESH,
    )
    swap.start()
    for dx, dc in others:
        exchange(dx, dc).wait_send()
    panel_gather.end()
    gram_gather.end()
    for dx in far_first:
        contribute(dx).wait_send()
        spread(gram_row, gx_send, gx_recv, dx).wait_send()
        spread(poly_row, px_send, px_recv, dx).wait_send()
    swap.wait_recv()
    for core in range(2):

        @pl.when(c == core)
        def _():
            out_ref[1 - core] = swap_in[...]

    swap.wait_send()


def solution(mesh):
    nx, groups = mesh.shape["mat"], mesh.shape["gr"]
    nz = nx
    ny = groups // nz

    def body(iterate):
        mats, _, rpd, total_cols = iterate.shape
        block_rows = rpd * nx * 2
        width = total_cols // nx
        gram_width = ny * block_rows
        dma = pltpu.SemaphoreType.DMA
        long = max(ny, nz)
        return pl.pallas_call(
            functools.partial(kernel, nx, nz, ny, total_cols),
            out_shape=jax.ShapeDtypeStruct((mats, block_rows, width // 2), jnp.bfloat16),
            in_specs=[pl.BlockSpec(memory_space=pl.ANY)],
            out_specs=pl.BlockSpec(memory_space=pltpu.VMEM),
            scratch_shapes=[
                pltpu.VMEM((nx, 2, rpd, width), jnp.bfloat16),
                pltpu.VMEM((block_rows, width), jnp.float32),
                pltpu.VMEM((nz, ny, block_rows, width), jnp.bfloat16),
                pltpu.VMEM((nx, block_rows, gram_width), jnp.float32),
                pltpu.VMEM((nx, block_rows, gram_width), jnp.float32),
                pltpu.VMEM((nz, ny, block_rows, gram_width), jnp.bfloat16),
                pltpu.VMEM((nx, block_rows, gram_width), jnp.bfloat16),
                pltpu.VMEM((nx, block_rows, gram_width), jnp.bfloat16),
                pltpu.VMEM((block_rows, width // 2), jnp.bfloat16),
                pltpu.VMEM((block_rows, width // 2), jnp.bfloat16),
                dma((nx, 2)),
                dma((nx, 2)),
                dma,
            ]
            + [dma((2, long))] * 2
            + [dma((2, long // 2, 2, 3))] * 2
            + [dma((2, long))] * 4
            + [dma((nx,))] * 6
            + [dma, dma],
            compiler_params=pltpu.CompilerParams(collective_id=0, has_side_effects=True),
        )(iterate.reshape(mats, rpd, total_cols))

    return jax.shard_map(
        body,
        mesh=mesh,
        in_specs=(P(None, "gr", ("mat", "gc"), None),),
        out_specs=P(None, "gr", ("mat", "gc")),
        check_vma=False,
    )
```

time: 111 us -> 93.9 us (0.85)
  Pallas kernels: 109 us -> 92.2 us
    pallas_call x1, Pallas kernels: 109 us -> 92.2 us  [body(): pl.pallas_call(functools.partial(kernel, nx, nz, ny, total_cols), out_sha...]
where the time goes in v2:
time: 93.9 us; the launch traced here: 93.7 us
  Pallas kernels  92.2 us (98%)
  local copies, waits for them, and re-layouts  1.47 us (2%)
    pallas_call x1, Pallas kernels, body(): pl.pallas_call(functools.partial(kernel, nx, nz, ny, total_cols), out_sha...  92.2 us

profile of v2, /device:TPU:1, one launch (start us, length us, event | category | flops | bytes accessed | tf_op | source)
XLA Modules:
  0.0 93.7 jit_solution(4247133489916450849)
XLA Ops:
  0.0 92.2 %shard_map.17 = bf16[2,32,448]{2,1,0:T(8,128)(2,1)} custom-call(bf16[2,2,7168]{2,1,0:T(2,128)(2,1)} %bitcast.1), custom_call_target="tpu_custom_call" | custom-call | tf_op jit(solution)/shard_map/pallas_call | solution.py:331
  92.2 1.5 %copy.3 = bf16[2,32,448]{2,1,0:T(8,128)(2,1)} copy(bf16[2,32,448]{2,1,0:T(8,128)(2,1)} %shard_map.17) | data formatting | bytes 114688

commit v3 on v2

--- a/solution.py
+++ b/solution.py
@@ -14,15 +14,52 @@
 quintic_coef = 2.0315
 
 
+def nearest_first(size):
+    return sorted(range(size), key=lambda d: 2 * d - 1 if d <= size // 2 else 2 * (size - d))
+
+
+def slot_of(d, size):
+    return nearest_first(size).index(d % size)
+
+
+def traced_slot(d, size):
+    return jnp.maximum(jnp.minimum(2 * d - 1, 2 * (size - d)), 0)
+
+
+def hop(size, d):
+    if size == 8 and d in (0, 3, 4, 5):
+        return {3: (-2, 1, None), 5: (2, -1, None), 4: (-2, 2, 0), 0: (2, -2, 1)}[d]
+    return 0, d, None
+
+
+def at_once(size):
+    return (2, 6, 1, 7) if size == 8 else tuple(range(1, size))
+
+
+def passed_on(size):
+    return (3, 5, 4, 0) if size == 8 else ()
+
+
+def line_copies(size):
+    return at_once(size) + passed_on(size)
+
+
+def arriving(size, place):
+    return [d for d in line_copies(size) if (hop(size, d)[0] - hop(size, d)[1] - place) % size == 0]
+
+
 class Gather:
     def __init__(self, buf, sizes, line, line_send, line_recv, send, recv):
         self.buf, self.sizes, self.line = buf, sizes, line
         self.line_send, self.line_recv, self.send, self.recv = line_send, line_recv, send, recv
         self.half_rows = buf.shape[2] // 2
 
-    def view(self, half, first, second):
+    def view(self, half, first, second, part=None):
         rows = pl.ds(half * self.half_rows, self.half_rows)
-        return self.buf.at[(second, first, rows) if half == 0 else (first, second, rows)]
+        width = self.buf.shape[3]
+        cut = (width // 128 + 1) // 2 * 128
+        columns = pl.ds(0, width) if part is None else pl.ds(cut, width - cut) if part else pl.ds(0, cut)
+        return self.buf.at[(second, first, rows, columns) if half == 0 else (first, second, rows, columns)]
 
     def first_size(self, half):
         return self.sizes[1 - half]
@@ -32,46 +69,57 @@
 
     def first_copy(self, half, d):
         size = self.first_size(half)
-        return pltpu.make_async_remote_copy(
-            src_ref=self.view(half, 0, 0),
-            dst_ref=self.view(half, size - d, 0),
+        source, to, part = hop(size, d)
+        return pltpu.make_async_remote_copy(
+            src_ref=self.view(half, slot_of(source, size), 0, part),
+            dst_ref=self.view(half, slot_of(source - to, size), 0, part),
             send_sem=self.line_send.at[half, d],
             recv_sem=self.line_recv.at[half, d],
-            device_id={"gr": self.line[1 - half][d]},
+            device_id={"gr": self.line[1 - half][to % size]},
             device_id_type=MESH,
         )
 
     def start_first(self):
-        for half in range(2):
-            for d in nearest_last(self.first_size(half)):
+        for n in range(max(self.sizes)):
+            for half in range(2):
+                now = at_once(self.first_size(half))
+                if n < len(now):
+                    self.first_copy(half, now[n]).start()
+
+    def wait_first(self, low, high):
+        for half in range(2):
+            size = self.first_size(half)
+            for place in nearest_first(size)[low:high]:
+                for d in arriving(size, place):
+                    self.first_copy(half, d).wait_recv()
+
+    def pass_on_first(self):
+        for half in range(2):
+            for d in passed_on(self.first_size(half)):
                 self.first_copy(half, d).start()
 
-    def wait_first(self, half, low, high):
-        size = self.first_size(half)
-        for place in range(max(low, 1), high):
-            self.first_copy(half, size - place).wait_recv()
-
     def end_first(self):
         for half in range(2):
-            for d in range(1, self.first_size(half)):
+            for d in line_copies(self.first_size(half)):
                 self.first_copy(half, d).wait_send()
 
 
 class RingGather(Gather):
     def chunks(self, half):
         size = self.first_size(half)
-        cuts = [(0, 1), (1, size // 2), (size // 2, size)]
+        cuts = [(0, 1), (1, min(3, size)), (3, min(5, size)), (5, min(7, size)), (7, size)]
         return [(k, low, high) for k, (low, high) in enumerate(cuts) if low < high]
 
     def steps(self, half):
         return self.second_size(half) // 2
 
     def has(self, half, step, way, k):
-        return step < self.steps(half) or (step == self.steps(half) and way == k // 2)
+        return step < self.steps(half) or (step == self.steps(half) and way == (k in (2, 3)))
 
     def copy(self, half, step, way, chunk):
         size, (k, low, high) = self.second_size(half), chunk
-        source, target = (step - 1, step) if way else ((size - step + 1) % size, size - step)
+        source, target = (step - 1, step) if way else (1 - step, -step)
+        source, target = slot_of(source, size), slot_of(target, size)
         return pltpu.make_async_remote_copy(
             src_ref=self.view(half, pl.ds(low, high - low), source),
             dst_ref=self.view(half, pl.ds(low, high - low), target),
@@ -89,30 +137,41 @@
                         if self.has(half, step, way, chunk[0]):
                             yield half, step, way, chunk
 
-    def run(self):
-        def start(half, step, way, chunk):
-            if self.has(half, step, way, chunk[0]):
-                self.copy(half, step, way, chunk).start()
-
+    def begin(self, n):
         for half in range(2):
             for way in range(2):
-                start(half, 1, way, self.chunks(half)[0])
+                if n < len(self.chunks(half)) and self.has(half, 1, way, n):
+                    self.copy(half, 1, way, self.chunks(half)[n]).start()
+
+    def forward(self, step, n):
+        for half in range(2):
+            for way in range(2):
+                if n < len(self.chunks(half)) and self.has(half, step, way, n):
+                    chunk = self.chunks(half)[n]
+                    self.copy(half, step, way, chunk).wait_recv()
+                    if self.has(half, step + 1, way, n):
+                        self.copy(half, step + 1, way, chunk).start()
+
+    def run(self, ready):
         self.start_first()
-        for n in range(1, 3):
+        self.begin(0)
+        self.wait_first(3, 5)
+        self.pass_on_first()
+        self.wait_first(1, 3)
+        self.begin(1)
+        self.begin(2)
+        self.forward(1, 0)
+        self.wait_first(5, 7)
+        self.begin(3)
+        self.wait_first(7, 8)
+        self.begin(4)
+        for step in range(1, max(self.steps(0), self.steps(1)) + 1):
+            for n in range(step == 1, 5):
+                self.forward(step, n)
             for half in range(2):
-                if n < len(self.chunks(half)):
-                    chunk = self.chunks(half)[n]
-                    self.wait_first(half, chunk[1], chunk[2])
-                    for way in range(2):
-                        start(half, 1, way, chunk)
-        for step in range(1, max(self.steps(0), self.steps(1)) + 1):
-            for n in range(3):
-                for half in range(2):
-                    for way in range(2):
-                        if n < len(self.chunks(half)) and self.has(half, step, way, self.chunks(half)[n][0]):
-                            chunk = self.chunks(half)[n]
-                            self.copy(half, step, way, chunk).wait_recv()
-                            start(half, step + 1, way, chunk)
+                if step <= self.steps(half):
+                    for d in sorted({0, step, self.second_size(half) - step} if step == 1 else {step, self.second_size(half) - step}):
+                        ready(half, d)
 
     def end(self):
         self.end_first()
@@ -120,33 +179,61 @@
             self.copy(*one).wait_send()
 
 
-class LineGather(Gather):
-    def copy(self, half, d):
+class HopGather(Gather):
+    def chunks(self, half):
+        size = self.first_size(half)
+        return [(0, min(5, size)), (5, size)][: 1 + (size > 5)]
+
+    def copy(self, half, d, k):
         size = self.second_size(half)
-        return pltpu.make_async_remote_copy(
-            src_ref=self.view(half, pl.ds(0, self.first_size(half)), 0),
-            dst_ref=self.view(half, pl.ds(0, self.first_size(half)), size - d),
-            send_sem=self.send.at[half, d],
-            recv_sem=self.recv.at[half, d],
-            device_id={"gr": self.line[half][d]},
+        source, to, part = hop(size, d)
+        low, high = self.chunks(half)[k]
+        return pltpu.make_async_remote_copy(
+            src_ref=self.view(half, pl.ds(low, high - low), slot_of(source, size), part),
+            dst_ref=self.view(half, pl.ds(low, high - low), slot_of(source - to, size), part),
+            send_sem=self.send.at[half, d, k],
+            recv_sem=self.recv.at[half, d, k],
+            device_id={"gr": self.line[half][to % size]},
             device_id_type=MESH,
         )
 
     def run(self):
+        waited = set()
+
+        def wait(half, d, k):
+            if (half, d, k) not in waited:
+                waited.add((half, d, k))
+                self.copy(half, d, k).wait_recv()
+
         self.start_first()
-        for half in range(2):
-            self.wait_first(half, 1, self.first_size(half))
-            for d in nearest_last(self.second_size(half)):
-                self.copy(half, d).start()
-        for half in range(2):
-            for d in nearest_last(self.second_size(half)):
-                self.copy(half, d).wait_recv()
+        self.wait_first(3, 5)
+        self.pass_on_first()
+        self.wait_first(1, 3)
+        for k in range(2):
+            if k:
+                self.wait_first(5, 8)
+            for half in range(2):
+                if k < len(self.chunks(half)):
+                    for d in at_once(self.second_size(half)):
+                        self.copy(half, d, k).start()
+        for k in range(2):
+            for half in range(2):
+                size = self.second_size(half)
+                for d in passed_on(size):
+                    for before in arriving(size, hop(size, d)[0]):
+                        wait(half, before, k)
+                    self.copy(half, d, k).start()
+        for half in range(2):
+            for k in range(len(self.chunks(half))):
+                for d in line_copies(self.second_size(half)):
+                    wait(half, d, k)
 
     def end(self):
         self.end_first()
         for half in range(2):
-            for d in range(1, self.second_size(half)):
-                self.copy(half, d).wait_send()
+            for k in range(len(self.chunks(half))):
+                for d in line_copies(self.second_size(half)):
+                    self.copy(half, d, k).wait_send()
 
 
 def nearest_last(size):
@@ -174,11 +261,19 @@
         [lax.rem(z + dz, nz) * ny + y for dz in range(nz)],
         [z * ny + lax.rem(y + dy, ny) for dy in range(ny)],
     )
-    place_z = [lax.rem(x_at[dx] + nz - z, nz) for dx in range(nx)]
-    place_y = [lax.rem(k + ny - y, ny) for k in range(ny)]
+    half_rows = block_rows // 2
+    slot_z = [traced_slot(lax.rem(k + nz - z, nz), nz) for k in range(nz)]
+    slot_y = [traced_slot(lax.rem(k + ny - y, ny), ny) for k in range(ny)]
+    block_z = [traced_slot(lax.rem(x_at[dx] + nz - z, nz), nz) for dx in range(nx)]
+    block_y = [traced_slot(lax.rem(x_at[dx] + ny - y, ny), ny) for dx in range(nx)]
+
+    def half_block(buf, half, slot):
+        if half == 0:
+            return jnp.concatenate([buf[slot, k, :half_rows] for k in slot_y], axis=0)
+        return jnp.concatenate([buf[k, slot, half_rows:] for k in slot_z], axis=0)
 
     def row_block(buf, dx):
-        return jnp.concatenate([buf[place_z[dx], place_y[k]] for k in range(ny)], axis=0)
+        return jnp.concatenate([half_block(buf, 0, block_z[dx]), half_block(buf, 1, block_y[dx])], axis=0)
 
     others = [(dx, dc) for dx in nearest_last(nx) + [0] for dc in range(2) if (dx, dc) != (0, 0)]
     barrier = pltpu.get_barrier_semaphore()
@@ -218,32 +313,55 @@
     block = assembled[...].astype(jnp.bfloat16)
     panel[0, 0] = block
 
+    def owner(half, d):
+        return lax.rem(z + d, nz) if half == 0 else lax.rem(y + d, ny)
+
+    def contribute(half, d):
+        return pltpu.make_async_remote_copy(
+            src_ref=partial.at[half, d],
+            dst_ref=partial_in.at[half, x],
+            send_sem=rs_send.at[half, d],
+            recv_sem=rs_recv.at[half, x],
+            device_id={"mat": owner(half, d)},
+            device_id_type=MESH,
+        )
+
+    def ready(half, d):
+        partial[half, d] = lax.dot_general(
+            block,
+            half_block(panel, half, slot_of(d, nx)),
+            (((1,), (1,)), ((), ())),
+            preferred_element_type=jnp.float32,
+        )
+
+        @pl.when(owner(half, d) != x)
+        def _():
+            contribute(half, d).start()
+
+        @pl.when(owner(half, d) == x)
+        def _():
+            partial_in[half, x] = partial[half, d]
+
     panel_gather = RingGather(panel, (nz, ny), line, pa_send, pa_recv, pb_send, pb_recv)
-    panel_gather.run()
-
-    def contribute(dx):
-        return pltpu.make_async_remote_copy(
-            src_ref=partial.at[dx],
-            dst_ref=partial_in.at[nx - dx],
-            send_sem=rs_send.at[dx],
-            recv_sem=rs_recv.at[dx],
-            device_id={"mat": x_at[dx]},
-            device_id_type=MESH,
-        )
+    panel_gather.run(ready)
 
     far_first = nearest_last(nx)
-    for dx in far_first + [0]:
-        value = lax.dot_general(
-            block, row_block(panel, dx), (((1,), (1,)), ((), ())), preferred_element_type=jnp.float32
-        )
-        if dx:
-            partial[dx] = value
-            contribute(dx).start()
-        else:
-            gram_sum = value
-    for dx in far_first:
-        contribute(dx).wait_recv()
-        gram_sum = gram_sum + partial_in[nx - dx]
+    sums = []
+    for half in range(2):
+        for dx in far_first:
+            pltpu.make_async_remote_copy(
+                src_ref=partial_in.at[half, x_at[dx]],
+                dst_ref=partial_in.at[half, x_at[dx]],
+                send_sem=rs_send.at[half, dx],
+                recv_sem=rs_recv.at[half, x_at[dx]],
+                device_id={"mat": x_at[dx]},
+                device_id_type=MESH,
+            ).wait_recv()
+        total = partial_in[half, 0]
+        for k in range(1, nx):
+            total = total + partial_in[half, k]
+        sums.append(total)
+    gram_sum = jnp.concatenate(sums, axis=1)
     gram = (gram_sum * (1.0 / total_cols)).astype(jnp.bfloat16)
     gram_row[0] = gram
     gram_cols[0, 0] = gram
@@ -260,7 +378,7 @@
 
     for dx in far_first:
         spread(gram_row, gx_send, gx_recv, dx).start()
-    gram_gather = LineGather(gram_cols, (nz, ny), line, ga_send, ga_recv, gb_send, gb_recv)
+    gram_gather = HopGather(gram_cols, (nz, ny), line, ga_send, ga_recv, gb_send, gb_recv)
     gram_gather.run()
     for dx in far_first:
         spread(gram_row, gx_send, gx_recv, dx).wait_recv()
@@ -302,8 +420,14 @@
         exchange(dx, dc).wait_send()
     panel_gather.end()
     gram_gather.end()
+    for half in range(2):
+        for d in range(nx):
+
+            @pl.when(owner(half, d) != x)
+            def _():
+                contribute(half, d).wait_send()
+
     for dx in far_first:
-        contribute(dx).wait_send()
         spread(gram_row, gx_send, gx_recv, dx).wait_send()
         spread(poly_row, px_send, px_recv, dx).wait_send()
     swap.wait_recv()
@@ -337,8 +461,8 @@
                 pltpu.VMEM((nx, 2, rpd, width), jnp.bfloat16),
                 pltpu.VMEM((block_rows, width), jnp.float32),
                 pltpu.VMEM((nz, ny, block_rows, width), jnp.bfloat16),
-                pltpu.VMEM((nx, block_rows, gram_width), jnp.float32),
-                pltpu.VMEM((nx, block_rows, gram_width), jnp.float32),
+                pltpu.VMEM((2, nx, block_rows, gram_width // 2), jnp.float32),
+                pltpu.VMEM((2, nx, block_rows, gram_width // 2), jnp.float32),
                 pltpu.VMEM((nz, ny, block_rows, gram_width), jnp.bfloat16),
                 pltpu.VMEM((nx, block_rows, gram_width), jnp.bfloat16),
                 pltpu.VMEM((nx, block_rows, gram_width), jnp.bfloat16),
@@ -349,9 +473,11 @@
                 dma,
             ]
             + [dma((2, long))] * 2
-            + [dma((2, long // 2, 2, 3))] * 2
-            + [dma((2, long))] * 4
-            + [dma((nx,))] * 6
+            + [dma((2, long // 2, 2, 5))] * 2
+            + [dma((2, long))] * 2
+            + [dma((2, long, 2))] * 2
+            + [dma((2, nx))] * 2
+            + [dma((nx,))] * 4
             + [dma, dma],
             compiler_params=pltpu.CompilerParams(collective_id=0, has_side_effects=True),
         )(iterate.reshape(mats, rpd, total_cols))

time: 93.9 us -> 89.2 us (0.950)
  Pallas kernels: 92.2 us -> 87.5 us
    pallas_call x1, Pallas kernels: 92.2 us -> 87.5 us  [body(): pl.pallas_call(functools.partial(kernel, nx, nz, ny, total_cols), out_sha...]
where the time goes in v3:
time: 89.2 us; the launch traced here: 89 us
  Pallas kernels  87.5 us (98%)
  local copies, waits for them, and re-layouts  1.47 us (2%)
    pallas_call x1, Pallas kernels, body(): pl.pallas_call(functools.partial(kernel, nx, nz, ny, total_cols), out_sha...  87.5 us

profile of v3, /device:TPU:1, one launch (start us, length us, event | category | flops | bytes accessed | tf_op | source)
XLA Modules:
  0.0 89.0 jit_solution(8926556769050293421)
XLA Ops:
  0.0 87.5 %shard_map.17 = bf16[2,32,448]{2,1,0:T(8,128)(2,1)} custom-call(bf16[2,2,7168]{2,1,0:T(2,128)(2,1)} %bitcast.1), custom_call_target="tpu_custom_call" | custom-call | tf_op jit(solution)/shard_map/pallas_call | solution.py:455
  87.5 1.5 %copy.3 = bf16[2,32,448]{2,1,0:T(8,128)(2,1)} copy(bf16[2,32,448]{2,1,0:T(8,128)(2,1)} %shard_map.17) | data formatting | bytes 114688

commit v4 on v3

--- a/solution.py
+++ b/solution.py
@@ -179,61 +179,66 @@
             self.copy(*one).wait_send()
 
 
-class HopGather(Gather):
-    def chunks(self, half):
+class LineGather(Gather):
+    relay = False
+
+    def first_copy(self, half, d):
         size = self.first_size(half)
-        return [(0, min(5, size)), (5, size)][: 1 + (size > 5)]
-
-    def copy(self, half, d, k):
+        return pltpu.make_async_remote_copy(
+            src_ref=self.view(half, 0, 0),
+            dst_ref=self.view(half, slot_of(-d, size), 0),
+            send_sem=self.line_send.at[half, d],
+            recv_sem=self.line_recv.at[half, d],
+            device_id={"gr": self.line[1 - half][d]},
+            device_id_type=MESH,
+        )
+
+    def plan(self, half):
         size = self.second_size(half)
-        source, to, part = hop(size, d)
-        low, high = self.chunks(half)[k]
-        return pltpu.make_async_remote_copy(
-            src_ref=self.view(half, pl.ds(low, high - low), slot_of(source, size), part),
-            dst_ref=self.view(half, pl.ds(low, high - low), slot_of(source - to, size), part),
-            send_sem=self.send.at[half, d, k],
-            recv_sem=self.recv.at[half, d, k],
+        if self.relay and size == 8:
+            return (2, 6, 3, 5, 1, 7), ((4, 2), (0, 6))
+        return tuple(nearest_last(size)), ()
+
+    def copy(self, half, d):
+        size = self.second_size(half)
+        relayed = [one for one, _ in self.plan(half)[1]]
+        source, to, part = hop(size, d) if d in relayed else (0, d, None)
+        return pltpu.make_async_remote_copy(
+            src_ref=self.view(half, pl.ds(0, self.first_size(half)), slot_of(source, size), part),
+            dst_ref=self.view(half, pl.ds(0, self.first_size(half)), slot_of(source - to, size), part),
+            send_sem=self.send.at[half, d],
+            recv_sem=self.recv.at[half, d],
             device_id={"gr": self.line[half][to % size]},
             device_id_type=MESH,
         )
 
     def run(self):
-        waited = set()
-
-        def wait(half, d, k):
-            if (half, d, k) not in waited:
-                waited.add((half, d, k))
-                self.copy(half, d, k).wait_recv()
-
-        self.start_first()
-        self.wait_first(3, 5)
-        self.pass_on_first()
-        self.wait_first(1, 3)
-        for k in range(2):
-            if k:
-                self.wait_first(5, 8)
-            for half in range(2):
-                if k < len(self.chunks(half)):
-                    for d in at_once(self.second_size(half)):
-                        self.copy(half, d, k).start()
-        for k in range(2):
-            for half in range(2):
-                size = self.second_size(half)
-                for d in passed_on(size):
-                    for before in arriving(size, hop(size, d)[0]):
-                        wait(half, before, k)
-                    self.copy(half, d, k).start()
-        for half in range(2):
-            for k in range(len(self.chunks(half))):
-                for d in line_copies(self.second_size(half)):
-                    wait(half, d, k)
+        for half in range(2):
+            for d in nearest_last(self.first_size(half)):
+                self.first_copy(half, d).start()
+        for half in range(2):
+            for d in range(1, self.first_size(half)):
+                self.first_copy(half, d).wait_recv()
+            for d in self.plan(half)[0]:
+                self.copy(half, d).start()
+        for half in range(2):
+            for d, before in self.plan(half)[1]:
+                self.copy(half, before).wait_recv()
+                self.copy(half, d).start()
+        for half in range(2):
+            now, later = self.plan(half)
+            relays = [before for _, before in later]
+            for d in now + tuple(d for d, _ in later):
+                if d not in relays:
+                    self.copy(half, d).wait_recv()
 
     def end(self):
-        self.end_first()
-        for half in range(2):
-            for k in range(len(self.chunks(half))):
-                for d in line_copies(self.second_size(half)):
-                    self.copy(half, d, k).wait_send()
+        for half in range(2):
+            for d in range(1, self.first_size(half)):
+                self.first_copy(half, d).wait_send()
+            now, later = self.plan(half)
+            for d in now + tuple(d for d, _ in later):
+                self.copy(half, d).wait_send()
 
 
 def nearest_last(size):
@@ -267,13 +272,15 @@
     block_z = [traced_slot(lax.rem(x_at[dx] + nz - z, nz), nz) for dx in range(nx)]
     block_y = [traced_slot(lax.rem(x_at[dx] + ny - y, ny), ny) for dx in range(nx)]
 
-    def half_block(buf, half, slot):
+    def half_block(buf, half, slot, columns=slice(None)):
         if half == 0:
-            return jnp.concatenate([buf[slot, k, :half_rows] for k in slot_y], axis=0)
-        return jnp.concatenate([buf[k, slot, half_rows:] for k in slot_z], axis=0)
-
-    def row_block(buf, dx):
-        return jnp.concatenate([half_block(buf, 0, block_z[dx]), half_block(buf, 1, block_y[dx])], axis=0)
+            return jnp.concatenate([buf[slot, k, :half_rows, columns] for k in slot_y], axis=0)
+        return jnp.concatenate([buf[k, slot, half_rows:, columns] for k in slot_z], axis=0)
+
+    def row_block(buf, dx, columns=slice(None)):
+        return jnp.concatenate(
+            [half_block(buf, 0, block_z[dx], columns), half_block(buf, 1, block_y[dx], columns)], axis=0
+        )
 
     others = [(dx, dc) for dx in nearest_last(nx) + [0] for dc in range(2) if (dx, dc) != (0, 0)]
     barrier = pltpu.get_barrier_semaphore()
@@ -378,7 +385,7 @@
 
     for dx in far_first:
         spread(gram_row, gx_send, gx_recv, dx).start()
-    gram_gather = HopGather(gram_cols, (nz, ny), line, ga_send, ga_recv, gb_send, gb_recv)
+    gram_gather = LineGather(gram_cols, (nz, ny), line, ga_send, ga_recv, gb_send, gb_recv)
     gram_gather.run()
     for dx in far_first:
         spread(gram_row, gx_send, gx_recv, dx).wait_recv()
@@ -390,22 +397,30 @@
     for dx in far_first:
         spread(poly_row, px_send, px_recv, dx).start()
 
-    mixed = jnp.zeros((block_rows, width), jnp.float32)
-    for dx in [0] + far_first[::-1]:
-        if dx:
-            spread(poly_row, px_send, px_recv, nx - dx).wait_recv()
-        mixed = mixed + jnp.dot(poly_row[dx], row_block(panel, dx), preferred_element_type=jnp.float32)
-    result = linear_coef * block.astype(jnp.float32) + mixed
-    halves = [
-        result[:, : width // 2].astype(jnp.bfloat16),
-        result[:, width // 2 :].astype(jnp.bfloat16),
-    ]
-    for core in range(2):
-
-        @pl.when(c == core)
-        def _():
-            out_ref[core] = halves[core]
-            swap_out[...] = halves[1 - core]
+    half_width = width // 2
+    low = half_width // 128 * 128
+    high = width - low
+
+    def product(start, size, arrives):
+        columns = pl.ds(pl.multiple_of(start, 128), size)
+        mixed = linear_coef * panel[0, 0, :, columns].astype(jnp.float32)
+        for dx in [0] + far_first[::-1]:
+            if dx and arrives:
+                spread(poly_row, px_send, px_recv, nx - dx).wait_recv()
+            mixed = mixed + jnp.dot(
+                poly_row[dx], row_block(panel, dx, columns), preferred_element_type=jnp.float32
+            )
+        return mixed
+
+    first_part = product((1 - c) * low, high, True)
+
+    @pl.when(c == 0)
+    def _():
+        swap_out[...] = first_part[:, half_width - low :].astype(jnp.bfloat16)
+
+    @pl.when(c == 1)
+    def _():
+        swap_out[...] = first_part[:, :half_width].astype(jnp.bfloat16)
 
     swap = pltpu.make_async_remote_copy(
         src_ref=swap_out,
@@ -416,6 +431,18 @@
         device_id_type=MESH,
     )
     swap.start()
+    second_part = product(c * high, low, False)
+
+    @pl.when(c == 0)
+    def _():
+        own_half = jnp.concatenate([second_part, first_part[:, : half_width - low]], axis=1)
+        out_ref[0] = own_half.astype(jnp.bfloat16)
+
+    @pl.when(c == 1)
+    def _():
+        own_half = jnp.concatenate([first_part[:, half_width:], second_part], axis=1)
+        out_ref[1] = own_half.astype(jnp.bfloat16)
+
     for dx, dc in others:
         exchange(dx, dc).wait_send()
     panel_gather.end()
@@ -474,8 +501,7 @@
             ]
             + [dma((2, long))] * 2
             + [dma((2, long // 2, 2, 5))] * 2
-            + [dma((2, long))] * 2
-            + [dma((2, long, 2))] * 2
+            + [dma((2, long))] * 4
             + [dma((2, nx))] * 2
             + [dma((nx,))] * 4
             + [dma, dma],

time: 89.2 us -> 87.2 us (0.978)
  Pallas kernels: 87.5 us -> 85.5 us
    pallas_call x1, Pallas kernels: 87.5 us -> 85.5 us  [body(): pl.pallas_call(functools.partial(kernel, nx, nz, ny, total_cols), out_sha...]
where the time goes in v4:
time: 87.2 us; the launch traced here: 86.9 us
  Pallas kernels  85.5 us (98%)
  local copies, waits for them, and re-layouts  1.47 us (2%)
    pallas_call x1, Pallas kernels, body(): pl.pallas_call(functools.partial(kernel, nx, nz, ny, total_cols), out_sha...  85.5 us

profile of v4, /device:TPU:1, one launch (start us, length us, event | category | flops | bytes accessed | tf_op | source)
XLA Modules:
  0.0 86.9 jit_solution(1180153049776234581)
XLA Ops:
  0.0 85.5 %shard_map.17 = bf16[2,32,448]{2,1,0:T(8,128)(2,1)} custom-call(bf16[2,2,7168]{2,1,0:T(2,128)(2,1)} %bitcast.1), custom_call_target="tpu_custom_call" | custom-call | tf_op jit(solution)/shard_map/pallas_call | solution.py:482
  85.5 1.5 %copy.3 = bf16[2,32,448]{2,1,0:T(8,128)(2,1)} copy(bf16[2,32,448]{2,1,0:T(8,128)(2,1)} %shard_map.17) | data formatting | bytes 114688
